TPU v7x, 128 devices: a whole 4x4x4 slice. The times are simulated.
128 devices in a mesh: prow: 16 (over z, x), pcol: 8 (over y, core).
Axes of the slice: x: 4, y: 4, z: 4, core: 2. Of those that a mesh axis runs over, the one named last changes fastest.
Arguments:
- kernel_tiles: float32 [4, 16, 256, 8, 8, 256], P(None, 'prow', None, None, 'pcol'), may hold values from 0 to 11, as said below
Outputs:
- factored: float32 [4, 16, 256, 8, 8, 256], P(None, 'prow', None, None, 'pcol')
Inputs may be any that keep to these rules, and one draw needn't show every extreme that they name: kernel_tiles is a symmetric positive definite matrix in the stated layout: a product of two exponential covariances of locations and times, scaled per point, plus a diagonal term of at least 0.5.
All inputs are finite; a program needn't handle non-finite values.
Results may differ from a plain program's by a relative error of at most 0.000061.
Values sent between devices are 32-bit elements; how exact they have to be, the bound alone decides.
A program may use at most 128 MiB of HBM per device.

v0:
```python
import jax
import jax.numpy as jnp
from jax import lax
from jax.sharding import PartitionSpec as P

highest = lax.Precision.HIGHEST


def picked(shard, axis, root):
    return lax.dynamic_index_in_dim(lax.all_gather(shard, axis), root, 0, keepdims=False)


def from_root(shard, axis, root):
    mine = lax.axis_index(axis) == root
    return lax.psum(jnp.where(mine, shard, jnp.zeros_like(shard)), axis)


def tile_solve(factor, tile_rows):
    tile_count, tile_width, _ = tile_rows.shape
    flat_rows = tile_rows.reshape(tile_count * tile_width, tile_width)
    solved = jax.scipy.linalg.solve_triangular(factor, flat_rows.T, lower=True)
    return solved.T.reshape(tile_count, tile_width, tile_width)


def factor_panel(local_block, panel_index, global_rows):
    procs_row = lax.axis_size("prow")
    procs_col = lax.axis_size("pcol")
    tile_row = panel_index // procs_row
    tile_col = panel_index // procs_col
    factor = jnp.linalg.cholesky(local_block[tile_row, :, tile_col, :])
    factor = picked(factor, "prow", panel_index % procs_row)
    solved = tile_solve(factor, local_block[:, :, tile_col, :])
    lower_rows = (global_rows > panel_index)[:, None, None]
    diag_rows = (global_rows == panel_index)[:, None, None]
    panel = jnp.where(lower_rows, solved, jnp.where(diag_rows, factor[None], jnp.float32(0.0)))
    row_panel = picked(panel, "pcol", panel_index % procs_col)
    return (panel, row_panel)


def column_tiles(row_panel):
    procs_row = lax.axis_size("prow")
    tile_width = row_panel.shape[1]
    procs_col = lax.axis_size("pcol")
    multiple = procs_row // procs_col
    col_index = lax.axis_index("pcol")
    received = []
    for owner_step in range(multiple):
        received.append(from_root(row_panel, "prow", col_index + owner_step * procs_col))
    stacked = jnp.stack(received, axis=1)
    return stacked.reshape(-1, tile_width, tile_width)


def trailing(local_block, lead, global_rows, global_cols, row_panel, col_panel):
    update = jnp.einsum("arn,csn->arcs", row_panel, col_panel, precision=highest)
    active = (global_rows > lead)[:, None, None, None] & (global_cols > lead)[None, None, :, None]
    return jnp.where(active, local_block - update, local_block)


def write_panel(local_block, panel_index, panel, global_rows, global_cols):
    in_column = (global_cols == panel_index)[None, None, :, None]
    result = jnp.where(in_column, panel[:, :, None, :], local_block)
    upper = (global_rows == panel_index)[:, None, None, None] & (global_cols > panel_index)[
        None, None, :, None
    ]
    return jnp.where(upper, jnp.float32(0.0), result)


def shards(kernel_tiles):
    row_count, _, tile_width, col_count, _, _ = kernel_tiles.shape
    local_block = kernel_tiles.reshape(row_count, tile_width, col_count, tile_width)
    global_rows = jnp.arange(row_count, dtype=jnp.int32) * lax.axis_size("prow") + lax.axis_index(
        "prow"
    )
    global_cols = jnp.arange(col_count, dtype=jnp.int32) * lax.axis_size("pcol") + lax.axis_index(
        "pcol"
    )
    panel_zero, rows_zero = factor_panel(local_block, 0, global_rows)
    cols_zero = column_tiles(rows_zero)
    result = trailing(local_block, 0, global_rows, global_cols, rows_zero, cols_zero)
    result = write_panel(result, 0, panel_zero, global_rows, global_cols)
    panel_one, rows_one = factor_panel(result, 1, global_rows)
    cols_one = column_tiles(rows_one)
    result = trailing(result, 1, global_rows, global_cols, rows_one, cols_one)
    result = write_panel(result, 1, panel_one, global_rows, global_cols)
    return result.reshape(kernel_tiles.shape)


def solution(mesh):
    in_specs = (P(None, "prow", None, None, "pcol", None),)
    out_specs = P(None, "prow", None, None, "pcol", None)
    return jax.shard_map(shards, mesh=mesh, in_specs=in_specs, out_specs=out_specs, check_vma=False)
```

profile of v0, /device:TPU:0, one launch (start us, length us, event | category | flops | bytes accessed | tf_op | source)
XLA Modules:
  0.0 611.4 jit_solution(7833220030949401913)
XLA Ops:
  6.5 20.5 %copy.31 = f32[4,1,256,8,1,256]{2,5,3,0,4,1:T(8,128)} copy(f32[4,1,256,8,1,256]{5,4,3,2,1,0:T(1,128)} %param.4) | data formatting | bytes 16777216 | tf_op args[0]
  27.1 1.0 slice_bitcast_fusion.1
  28.2 1.0 fusion.18
  29.2 11.7 %cholesky.130 = f32[128,128]{1,0:T(8,128)S(1)} custom-call(f32[128,128]{1,0:T(8,128)S(1)} %cholesky.194), custom_call_target="Cholesky" | custom-call | tf_op jit(solution)/shard_map/jit(cholesky)/cholesky | solution.py:30
  41.0 9.8 %custom-call.13 = f32[1,128,128]{1,2,0:T(8,128)S(1)} custom-call(f32[1,128,128]{2,1,0:T(8,128)S(1)} %get-tuple-element.62), custom_call_target="InvertDiagBlocksLowerTriangular" | custom-call | tf_op jit(solution)/shard_map/jit(cholesky)/cholesky | solution.py:30
  51.0 0.3 convolution_subtract_fusion.3
  51.3 11.7 %cholesky.147 = f32[128,128]{1,0:T(8,128)S(1)} custom-call(f32[128,128]{1,0:T(8,128)S(1)} %convolution_subtract_fusion.3), custom_call_target="Cholesky" | custom-call | tf_op jit(solution)/shard_map/jit(cholesky)/cholesky | solution.py:30
  63.0 0.7 compare_reduce_fusion.2
  64.9 0.7 fusion.19
  65.6 0.5 all-gather.7.cloned.1.call-start
  66.1 1.3 slice.70
  67.5 0.3 copy.33
  67.8 0.3 copy.34
  68.2 51.7 %all-gather.11.cloned.1.call-done = f32[4096,256]{1,0:T(8,128)} async-done(((f32[256,256]{1,0:T(8,128)}), f32[4096,256]{1,0:T(8,128)}) %all-gather.11.cloned.1.call-update) | async-done | bytes 4194320 | tf_op jit(solution)/shard_map/all_gather | solution.py:10
  119.9 1.0 fusion.40
  121.0 3.8 while.4
  121.0 0.6 fusion.53
  121.6 1.3 bitcast_dynamic-update-slice_fusion.4
  122.9 0.6 fusion.53
  123.5 1.3 bitcast_dynamic-update-slice_fusion.4
  124.8 19.7 %custom-call.14 = f32[2,128,128]{1,2,0:T(8,128)S(1)} custom-call(f32[2,128,128]{2,1,0:T(8,128)S(1)} %get-tuple-element.21), custom_call_target="InvertDiagBlocksLowerTriangular" | custom-call | tf_op jit(solution)/shard_map/jit(_solve_triangular)/triangular_solve | solution.py:21
  144.5 0.6 fusion.15
  145.1 0.6 convolution_subtract_fusion.1
  145.7 0.6 fusion.28
  146.5 0.3 copy.53
  146.8 1.3 select_select_fusion.2
  148.1 49.4 %all-gather.7.cloned.1.call-done = f32[8,4,256,256]{3,2,1,0:T(8,128)} async-done(((f32[1,4,256,256]{3,2,1,0:T(8,128)}), f32[8,4,256,256]{3,2,1,0:T(8,128)}) %all-gather.7.cloned.1.call-update) | async-done | bytes 8388624 | tf_op jit(solution)/shard_map/all_gather | solution.py:10
  197.5 2.8 fusion.9
  200.7 0.3 copy.36
  201.0 90.6 %all-reduce.8.cloned.1.call-done = (f32[4,1,256,256]{3,2,0,1:T(8,128)}, f32[4,1,256,256]{3,2,0,1:T(8,128)}) async-done(((f32[4,1,256,256]{3,2,0,1:T(8,128)}, f32[4,1,256,256]{3,2,0,1:T(8,128)}), (f32[4,1,256,256]{3,2,0,1:T(8,128)}, f32[4,1,256,256]{3,2,0,1:T(8,128)})) %all-reduce.8.cloned.1.call-update) | async-done | bytes 2097168 | tf_op jit(solution)/shard_map/psum | solution.py:15
  291.6 1.7 pad_maximum_fusion
  293.4 11.1 %fusion.1 = f32[4,256,8,256]{1,3,2,0:T(8,128)S(1)} fusion(f32[4,256,256]{1,2,0:T(8,128)S(1)} %copy.36, pred[8]{0:T(512)(128)(4,1)S(1)} %broadcast_compare_fusion, pred[4,8]{1,0:T(4,128)(4,1)S(1)} %get-tuple-element.66, pred[4,8]{1,0:T(4,128)(4,1)S(1)} %get-tuple-element.65, f32[8,256,256,1]{2,1,0,3:T(8,128)S(1)} %bitcast.131, ...), kind=kOutput, calls=%fused_computation.7 | convolution fusion | flops 6450839552 | bytes 20971592 | tf_op jit(solution)/shard_map/arn,csn->arcs/dot_general | solution.py:54
  304.5 3.4 copy-done
  308.1 1.0 fusion.17
  309.1 11.7 %cholesky.164 = f32[128,128]{1,0:T(8,128)S(1)} custom-call(f32[128,128]{1,0:T(8,128)S(1)} %cholesky.197), custom_call_target="Cholesky" | custom-call | tf_op jit(solution)/shard_map/jit(cholesky)/cholesky | solution.py:30
  320.8 9.8 %custom-call.15 = f32[1,128,128]{1,2,0:T(8,128)S(1)} custom-call(f32[1,128,128]{2,1,0:T(8,128)S(1)} %get-tuple-element.58), custom_call_target="InvertDiagBlocksLowerTriangular" | custom-call | tf_op jit(solution)/shard_map/jit(cholesky)/cholesky | solution.py:30
  330.9 0.3 convolution_subtract_fusion.2
  331.1 11.7 %cholesky.181 = f32[128,128]{1,0:T(8,128)S(1)} custom-call(f32[128,128]{1,0:T(8,128)S(1)} %convolution_subtract_fusion.2), custom_call_target="Cholesky" | custom-call | tf_op jit(solution)/shard_map/jit(cholesky)/cholesky | solution.py:30
  342.9 0.6 compare_reduce_fusion.1
  343.5 0.7 compare_reduce_fusion
  345.4 0.7 fusion.21
  346.2 1.3 slice.73
  347.5 0.3 copy.41
  347.9 0.3 copy.42
  348.2 49.3 %all-gather.13.cloned.1.call-done = f32[4096,256]{1,0:T(8,128)} async-done(((f32[256,256]{1,0:T(8,128)}), f32[4096,256]{1,0:T(8,128)}) %all-gather.13.cloned.1.call-update) | async-done | bytes 4194320 | tf_op jit(solution)/shard_map/all_gather | solution.py:10
  397.5 1.0 fusion.39
  398.5 4.0 while.5
  398.7 0.6 fusion.54
  399.3 1.3 bitcast_dynamic-update-slice_fusion.5
  400.6 0.6 fusion.54
  401.2 1.3 bitcast_dynamic-update-slice_fusion.5
  402.5 19.7 %custom-call.16 = f32[2,128,128]{1,2,0:T(8,128)S(1)} custom-call(f32[2,128,128]{2,1,0:T(8,128)S(1)} %get-tuple-element.22), custom_call_target="InvertDiagBlocksLowerTriangular" | custom-call | tf_op jit(solution)/shard_map/jit(_solve_triangular)/triangular_solve | solution.py:21
  422.2 0.6 fusion.13
  422.8 0.6 convolution_subtract_fusion
  423.4 0.6 fusion.24
  424.2 0.3 copy.43
  424.5 1.3 select_select_fusion
  425.8 49.4 %all-gather.9.cloned.1.call-done = f32[8,4,256,256]{3,2,1,0:T(8,128)} async-done(((f32[1,4,256,256]{3,2,1,0:T(8,128)}), f32[8,4,256,256]{3,2,1,0:T(8,128)}) %all-gather.9.cloned.1.call-update) | async-done | bytes 8388624 | tf_op jit(solution)/shard_map/all_gather | solution.py:10
  475.2 2.8 fusion.7
  478.3 0.3 copy.44
  478.6 90.9 %all-reduce.6.cloned.1.call-done = (f32[4,1,256,256]{3,2,0,1:T(8,128)}, f32[4,1,256,256]{3,2,0,1:T(8,128)}) async-done(((f32[4,1,256,256]{3,2,0,1:T(8,128)}, f32[4,1,256,256]{3,2,0,1:T(8,128)}), (f32[4,1,256,256]{3,2,0,1:T(8,128)}, f32[4,1,256,256]{3,2,0,1:T(8,128)})) %all-reduce.6.cloned.1.call-update) | async-done | bytes 2097168 | tf_op jit(solution)/shard_map/psum | solution.py:15
  569.5 1.7 pad_maximum_fusion.1
  571.4 12.4 %fusion.4 = f32[4,1,256,8,1,256]{2,5,3,0,4,1:T(8,128)} fusion(f32[4,256,8,256]{1,3,2,0:T(8,128)} %copy-done, f32[4,256,256]{1,2,0:T(8,128)S(1)} %copy.44, pred[8]{0:T(512)(128)(4,1)S(1)} %broadcast_compare_fusion.4, pred[4,8]{1,0:T(4,128)(4,1)S(1)} %get-tuple-element.64, pred[4,8]{1,0:T(4,128)(4,1)S(1)} %get-tuple-element.63, ...), kind=kOutput, calls=%fused_computation.10 | convolution fusion | flops 6450839552 | bytes 20971592 | tf_op jit(solution)/shard_map/arn,csn->arcs/dot_general | solution.py:54
  583.8 20.5 %copy.48 = f32[4,1,256,8,1,256]{5,4,3,2,1,0:T(1,128)} copy(f32[4,1,256,8,1,256]{2,5,3,0,4,1:T(8,128)} %fusion.4) | data formatting | bytes 16777216 | tf_op jit(solution)/shard_map/reshape | solution.py:85
  (46 shorter events, 2.3 us)
Async XLA Ops:
  6.5 113.4 %all-gather.11.cloned.1.call-start = ((), (), s32[]{:S(2)}) async-start(), calls=%async_computation.2 | async-start | bytes 4456448 | tf_op jit(solution)/shard_map/all_gather | solution.py:10
  65.6 131.9 %all-gather.7.cloned.1.call-start = ((), (), s32[]{:S(2)}) async-start(), calls=%async_computation | async-start | bytes 9437184 | tf_op jit(solution)/shard_map/all_gather | solution.py:10
  148.1 143.5 %all-reduce.8.cloned.1.call-start = ((), (), s32[]{:S(2)}) async-start(), calls=%async_computation.5 | async-start | bytes 4194304 | tf_op jit(solution)/shard_map/psum | solution.py:15
  200.3 197.1 %all-gather.13.cloned.1.call-start = ((), (), s32[]{:S(2)}) async-start(), calls=%async_computation.3 | async-start | bytes 4456448 | tf_op jit(solution)/shard_map/all_gather | solution.py:10
  304.5 3.4 copy-start
  346.1 129.1 %all-gather.9.cloned.1.call-start = ((), (), s32[]{:S(2)}) async-start(), calls=%async_computation.1 | async-start | bytes 9437184 | tf_op jit(solution)/shard_map/all_gather | solution.py:10
  425.8 143.7 %all-reduce.6.cloned.1.call-start = ((), (), s32[]{:S(2)}) async-start(), calls=%async_computation.4 | async-start | bytes 4194304 | tf_op jit(solution)/shard_map/psum | solution.py:15
Sparse Core Ops, SparseCore 0:
  65.8 54.1 all-gather.10
  148.2 49.2 all-gather.6
  201.0 90.5 all-reduce.7
  346.3 51.1 all-gather.12
  425.9 49.2 all-gather.8
  478.9 90.6 all-reduce.5
where the time goes:
time: 621 us; the launch traced here: 611 us
  waiting for transfers between devices  381 us (61%)
  other arithmetic  125 us (20%)
  local copies, waits for them, and re-layouts  58.9 us (9%)
  matrix products  28.1 us (5%)
  between operations  16.5 us (3%)
    all_gather x4, waiting for transfers between devices, picked(): lax.all_gather(shard, axis)  200 us
    psum x2, waiting for transfers between devices, from_root(): return lax.psum(jnp.where(mine, shard, jnp.zeros_like(shard)), axis)  181 us
    another operation x13, other arithmetic, factor_panel(): factor = jnp.linalg.cholesky(local_block[tile_row, :, tile_col, :])  68.6 us
    another operation x3, other arithmetic, tile_solve(): solved = jax.scipy.linalg.solve_triangular(factor, flat_rows.T, lower=True)  39.4 us
    unnamed x3, local copies, waits for them, and re-layouts  23.9 us
    dot_general x2, matrix products, trailing(): jnp.einsum('arn,csn->arcs', row_panel, col_panel, precision=highest)  23.5 us
    reshape x1, local copies, waits for them, and re-layouts, shards(): return result.reshape(kernel_tiles.shape)  20.5 us
  transfers between devices with their start and end apart: 6, of which 6 were waited for; matrix products, arithmetic and copies ran while one was open for 1% of the time, Pallas kernels for 0%

commit v1 on v0

--- a/solution.py
+++ b/solution.py
@@ -12,7 +12,7 @@
 
 def from_root(shard, axis, root):
     mine = lax.axis_index(axis) == root
-    return lax.psum(jnp.where(mine, shard, jnp.zeros_like(shard)), axis)
+    return jnp.sum(lax.all_gather(jnp.where(mine, shard, jnp.zeros_like(shard)), axis), axis=0)
 
 
 def tile_solve(factor, tile_rows):

time: 621 us -> 900 us (1.45)
  waiting for transfers between devices: 381 us -> 635 us
  other arithmetic: 125 us -> 151 us
    all_gather x0 -> x4, waiting for transfers between devices: none -> 434 us  [from_root(): lax.all_gather(jnp.where(mine, shard, jnp.zeros_like(shard)), axis)]
    psum x2 -> x0, waiting for transfers between devices: 181 us -> none  [from_root(): return lax.psum(jnp.where(mine, shard, jnp.zeros_like(shard)), axis)]
    reduce_sum x0 -> x4, other arithmetic: none -> 28 us  [from_root(): jnp.sum(lax.all_gather(jnp.where(mine, shard, jnp.zeros_like(shard)), axi...]
  transfers between devices with their start and end apart: 6 -> 8, of which waited for: 6 -> 8; matrix products, arithmetic and copies ran while one was open for 1% -> 2% of each run, Pallas kernels for 0% -> 0%
where the time goes in v1:
time: 900 us; the launch traced here: 890 us
  waiting for transfers between devices  635 us (71%)
  other arithmetic  151 us (17%)
  local copies, waits for them, and re-layouts  58.7 us (7%)
  matrix products  28.1 us (3%)
  between operations  16.7 us (2%)
    all_gather x4, waiting for transfers between devices, from_root(): lax.all_gather(jnp.where(mine, shard, jnp.zeros_like(shard)), axis)  434 us
    all_gather x4, waiting for transfers between devices, picked(): lax.all_gather(shard, axis)  200 us
    another operation x13, other arithmetic, factor_panel(): factor = jnp.linalg.cholesky(local_block[tile_row, :, tile_col, :])  68.7 us
    another operation x3, other arithmetic, tile_solve(): solved = jax.scipy.linalg.solve_triangular(factor, flat_rows.T, lower=True)  39.4 us
    reduce_sum x4, other arithmetic, from_root(): jnp.sum(lax.all_gather(jnp.where(mine, shard, jnp.zeros_like(shard)), axi...  28 us
    unnamed x3, local copies, waits for them, and re-layouts  23.9 us
    dot_general x2, matrix products, trailing(): jnp.einsum('arn,csn->arcs', row_panel, col_panel, precision=highest)  23.5 us
    reshape x1, local copies, waits for them, and re-layouts, shards(): return result.reshape(kernel_tiles.shape)  20.5 us
  transfers between devices with their start and end apart: 8, of which 8 were waited for; matrix products, arithmetic and copies ran while one was open for 2% of the time, Pallas kernels for 0%

profile of v1, /device:TPU:0, one launch (start us, length us, event | category | flops | bytes accessed | tf_op | source)
XLA Modules:
  0.0 890.2 jit_solution(53640242560959556)
XLA Ops:
  6.5 20.5 %copy.28 = f32[4,1,256,8,1,256]{2,5,3,0,4,1:T(8,128)} copy(f32[4,1,256,8,1,256]{5,4,3,2,1,0:T(1,128)} %param.4) | data formatting | bytes 16777216 | tf_op args[0]
  27.1 1.0 slice_bitcast_fusion.1
  28.2 1.0 fusion.14
  29.2 11.7 %cholesky.130 = f32[128,128]{1,0:T(8,128)S(1)} custom-call(f32[128,128]{1,0:T(8,128)S(1)} %cholesky.194), custom_call_target="Cholesky" | custom-call | tf_op jit(solution)/shard_map/jit(cholesky)/cholesky | solution.py:30
  41.0 9.8 %custom-call.13 = f32[1,128,128]{1,2,0:T(8,128)S(1)} custom-call(f32[1,128,128]{2,1,0:T(8,128)S(1)} %get-tuple-element.62), custom_call_target="InvertDiagBlocksLowerTriangular" | custom-call | tf_op jit(solution)/shard_map/jit(cholesky)/cholesky | solution.py:30
  51.3 11.7 %cholesky.147 = f32[128,128]{1,0:T(8,128)S(1)} custom-call(f32[128,128]{1,0:T(8,128)S(1)} %convolution_subtract_fusion.3), custom_call_target="Cholesky" | custom-call | tf_op jit(solution)/shard_map/jit(cholesky)/cholesky | solution.py:30
  63.0 0.7 compare_reduce_fusion.2
  65.0 0.7 fusion.15
  65.7 0.5 all-gather.11.cloned.1.call-start
  66.2 1.3 slice.70
  67.6 0.3 copy.30
  67.9 0.3 copy.31
  68.3 51.7 %all-gather.23.cloned.1.call-done = f32[4096,256]{1,0:T(8,128)} async-done(((f32[256,256]{1,0:T(8,128)}), f32[4096,256]{1,0:T(8,128)}) %all-gather.23.cloned.1.call-update) | async-done | bytes 4194320 | tf_op jit(solution)/shard_map/all_gather | solution.py:10
  120.0 1.0 fusion.38
  121.1 4.1 while.4
  121.1 0.6 fusion.51
  121.8 1.3 bitcast_dynamic-update-slice_fusion.4
  123.1 0.6 fusion.51
  123.8 1.3 bitcast_dynamic-update-slice_fusion.4
  125.2 19.7 %custom-call.14 = f32[2,128,128]{1,2,0:T(8,128)S(1)} custom-call(f32[2,128,128]{2,1,0:T(8,128)S(1)} %get-tuple-element.21), custom_call_target="InvertDiagBlocksLowerTriangular" | custom-call | tf_op jit(solution)/shard_map/jit(_solve_triangular)/triangular_solve | solution.py:21
  144.8 0.6 fusion.11
  145.5 0.6 convolution_subtract_fusion.1
  146.1 0.6 fusion.24
  147.0 0.3 copy.48
  147.3 1.2 select_select_fusion.1
  148.5 49.4 %all-gather.11.cloned.1.call-done = f32[8,4,256,256]{3,2,1,0:T(8,128)} async-done(((f32[1,4,256,256]{3,2,1,0:T(8,128)}), f32[8,4,256,256]{3,2,1,0:T(8,128)}) %all-gather.11.cloned.1.call-update) | async-done | bytes 8388624 | tf_op jit(solution)/shard_map/all_gather | solution.py:10
  197.9 2.8 slice_select_fusion.3
  200.8 0.5 all-gather.13.cloned.1.call-update
  201.8 110.7 %all-gather.15.cloned.1.call-done = f32[16,4,256,256]{3,2,1,0:T(8,128)} async-done(((f32[1,4,256,256]{3,2,1,0:T(8,128)}), f32[16,4,256,256]{3,2,1,0:T(8,128)}) %all-gather.15.cloned.1.call-update) | async-done | bytes 16777232 | tf_op jit(solution)/shard_map/all_gather | solution.py:15
  312.5 7.0 reduce_sum.37
  319.5 106.1 %all-gather.13.cloned.1.call-done = f32[16,4,256,256]{3,2,1,0:T(8,128)} async-done(((f32[1,4,256,256]{3,2,1,0:T(8,128)}), f32[16,4,256,256]{3,2,1,0:T(8,128)}) %all-gather.13.cloned.1.call-update) | async-done | bytes 16777232 | tf_op jit(solution)/shard_map/all_gather | solution.py:15
  425.6 7.0 reduce_sum.36
  432.8 11.1 %fusion.1 = f32[4,256,8,256]{1,3,2,0:T(8,128)S(1)} fusion(f32[4,256,256]{1,2,0:T(8,128)S(1)} %bitcast_select_fusion.1, pred[8]{0:T(512)(128)(4,1)S(1)} %broadcast_compare_fusion, pred[4,8]{1,0:T(4,128)(4,1)S(1)} %get-tuple-element.66, pred[4,8]{1,0:T(4,128)(4,1)S(1)} %get-tuple-element.65, f32[8,256,256,1]{2,1,0,3:T(8,128)S(1)} %bitcast.115, ...), kind=kOutput, calls=%fused_computation.7 | convolution fusion | flops 6450839552 | bytes 20971592 | tf_op jit(solution)/shard_map/arn,csn->arcs/dot_general | solution.py:54
  443.9 3.4 copy-done
  447.5 1.0 fusion.13
  448.5 11.7 %cholesky.164 = f32[128,128]{1,0:T(8,128)S(1)} custom-call(f32[128,128]{1,0:T(8,128)S(1)} %cholesky.197), custom_call_target="Cholesky" | custom-call | tf_op jit(solution)/shard_map/jit(cholesky)/cholesky | solution.py:30
  460.3 9.8 %custom-call.15 = f32[1,128,128]{1,2,0:T(8,128)S(1)} custom-call(f32[1,128,128]{2,1,0:T(8,128)S(1)} %get-tuple-element.58), custom_call_target="InvertDiagBlocksLowerTriangular" | custom-call | tf_op jit(solution)/shard_map/jit(cholesky)/cholesky | solution.py:30
  470.6 11.7 %cholesky.181 = f32[128,128]{1,0:T(8,128)S(1)} custom-call(f32[128,128]{1,0:T(8,128)S(1)} %convolution_subtract_fusion.2), custom_call_target="Cholesky" | custom-call | tf_op jit(solution)/shard_map/jit(cholesky)/cholesky | solution.py:30
  482.3 0.7 compare_reduce_fusion.1
  483.0 0.7 compare_reduce_fusion
  484.9 0.7 fusion.17
  485.8 1.3 slice.73
  487.7 49.3 %all-gather.25.cloned.1.call-done = f32[4096,256]{1,0:T(8,128)} async-done(((f32[256,256]{1,0:T(8,128)}), f32[4096,256]{1,0:T(8,128)}) %all-gather.25.cloned.1.call-update) | async-done | bytes 4194320 | tf_op jit(solution)/shard_map/all_gather | solution.py:10
  537.1 1.0 fusion.37
  538.1 4.3 while.5
  538.3 0.6 fusion.52
  539.0 1.3 bitcast_dynamic-update-slice_fusion.5
  540.4 0.6 fusion.52
  541.0 1.3 bitcast_dynamic-update-slice_fusion.5
  542.4 19.7 %custom-call.16 = f32[2,128,128]{1,2,0:T(8,128)S(1)} custom-call(f32[2,128,128]{2,1,0:T(8,128)S(1)} %get-tuple-element.22), custom_call_target="InvertDiagBlocksLowerTriangular" | custom-call | tf_op jit(solution)/shard_map/jit(_solve_triangular)/triangular_solve | solution.py:21
  562.1 0.6 fusion.9
  562.7 0.6 convolution_subtract_fusion
  563.3 0.6 fusion.20
  564.2 0.3 copy.41
  564.5 1.2 select_select_fusion
  565.8 49.4 %all-gather.17.cloned.1.call-done = f32[8,4,256,256]{3,2,1,0:T(8,128)} async-done(((f32[1,4,256,256]{3,2,1,0:T(8,128)}), f32[8,4,256,256]{3,2,1,0:T(8,128)}) %all-gather.17.cloned.1.call-update) | async-done | bytes 8388624 | tf_op jit(solution)/shard_map/all_gather | solution.py:10
  615.2 2.8 slice_select_fusion.1
  618.0 0.7 all-gather.19.cloned.1.call-update
  619.1 110.6 %all-gather.21.cloned.1.call-done = f32[16,4,256,256]{3,2,1,0:T(8,128)} async-done(((f32[1,4,256,256]{3,2,1,0:T(8,128)}), f32[16,4,256,256]{3,2,1,0:T(8,128)}) %all-gather.21.cloned.1.call-update) | async-done | bytes 16777232 | tf_op jit(solution)/shard_map/all_gather | solution.py:15
  729.8 7.0 reduce_sum.39
  736.8 106.2 %all-gather.19.cloned.1.call-done = f32[16,4,256,256]{3,2,1,0:T(8,128)} async-done(((f32[1,4,256,256]{3,2,1,0:T(8,128)}), f32[16,4,256,256]{3,2,1,0:T(8,128)}) %all-gather.19.cloned.1.call-update) | async-done | bytes 16777232 | tf_op jit(solution)/shard_map/all_gather | solution.py:15
  843.0 7.0 reduce_sum.38
  850.2 12.4 %fusion.4 = f32[4,1,256,8,1,256]{2,5,3,0,4,1:T(8,128)} fusion(f32[4,256,8,256]{1,3,2,0:T(8,128)} %copy-done, f32[4,256,256]{1,2,0:T(8,128)S(1)} %bitcast_select_fusion, pred[8]{0:T(512)(128)(4,1)S(1)} %broadcast_compare_fusion.4, pred[4,8]{1,0:T(4,128)(4,1)S(1)} %get-tuple-element.64, pred[4,8]{1,0:T(4,128)(4,1)S(1)} %get-tuple-element.63, ...), kind=kOutput, calls=%fused_computation.10 | convolution fusion | flops 6450839552 | bytes 20971592 | tf_op jit(solution)/shard_map/arn,csn->arcs/dot_general | solution.py:54
  862.6 20.5 %copy.43 = f32[4,1,256,8,1,256]{5,4,3,2,1,0:T(1,128)} copy(f32[4,1,256,8,1,256]{2,5,3,0,4,1:T(8,128)} %fusion.4) | data formatting | bytes 16777216 | tf_op jit(solution)/shard_map/reshape | solution.py:85
  (54 shorter events, 4.3 us)
Async XLA Ops:
  6.5 113.5 %all-gather.23.cloned.1.call-start = ((), (), s32[]{:S(2)}) async-start(), calls=%async_computation.6 | async-start | bytes 4456448 | tf_op jit(solution)/shard_map/all_gather | solution.py:10
  65.7 132.2 %all-gather.11.cloned.1.call-start = ((), (), s32[]{:S(2)}) async-start(), calls=%async_computation | async-start | bytes 9437184 | tf_op jit(solution)/shard_map/all_gather | solution.py:10
  148.5 164.1 %all-gather.15.cloned.1.call-start = ((), (), s32[]{:S(2)}) async-start(), calls=%async_computation.2 | async-start | bytes 17825792 | tf_op jit(solution)/shard_map/all_gather | solution.py:15
  200.8 224.9 %all-gather.13.cloned.1.call-start = ((), (), s32[]{:S(2)}) async-start(), calls=%async_computation.1 | async-start | bytes 17825792 | tf_op jit(solution)/shard_map/all_gather | solution.py:15
  201.3 335.8 %all-gather.25.cloned.1.call-start = ((), (), s32[]{:S(2)}) async-start(), calls=%async_computation.7 | async-start | bytes 4456448 | tf_op jit(solution)/shard_map/all_gather | solution.py:10
  443.9 3.4 copy-start
  485.7 129.5 %all-gather.17.cloned.1.call-start = ((), (), s32[]{:S(2)}) async-start(), calls=%async_computation.3 | async-start | bytes 9437184 | tf_op jit(solution)/shard_map/all_gather | solution.py:10
  565.7 164.1 %all-gather.21.cloned.1.call-start = ((), (), s32[]{:S(2)}) async-start(), calls=%async_computation.5 | async-start | bytes 17825792 | tf_op jit(solution)/shard_map/all_gather | solution.py:15
  618.0 225.0 %all-gather.19.cloned.1.call-start = ((), (), s32[]{:S(2)}) async-start(), calls=%async_computation.4 | async-start | bytes 17825792 | tf_op jit(solution)/shard_map/all_gather | solution.py:15
Sparse Core Ops, SparseCore 0:
  65.9 54.1 all-gather.22
  148.6 49.2 all-gather.10
  200.9 111.6 all-gather.14
  314.5 111.0 all-gather.12
  485.8 51.2 all-gather.24
  565.8 49.2 all-gather.16
  618.1 111.6 all-gather.20
  731.9 111.0 all-gather.18
